TPU v7x, 32 devices: a whole 2x2x4 slice. The times are simulated.
32 devices in a mesh: dp: 8 (over y, x, core), seq: 4 (over z).
Axes of the slice: x: 2, y: 2, z: 4, core: 2. Of those that a mesh axis runs over, the one named last changes fastest.
Arguments:
- tokens: bfloat16 [8, 512, 6, 768], P('dp', 'seq'), may hold values from -6 to 6
- kind: int32 [8], P('dp'), may hold values from 0 to 1, as said below
- ln1_gain: float32 [768], replicated, may hold values from 0.1 to 1.9
- w_in: bfloat16 [768, 2304], replicated, may hold values from -0.21875 to 0.21875
- short_taps: float32 [3, 2304], replicated, may hold values from -3 to 3
- cond_taps: float32 [3, 768], replicated, may hold values from -3 to 3
- w_cond: bfloat16 [768, 768], replicated, may hold values from -0.21875 to 0.21875
- cond_bias: float32 [768], replicated, may hold values from -3 to 3
- w_out: bfloat16 [768, 768], replicated, may hold values from -0.21875 to 0.21875
- ln2_gain: float32 [768], replicated, may hold values from 0.1 to 1.9
- w_gate: bfloat16 [768, 3072], replicated, may hold values from -0.21875 to 0.21875
- w_up: bfloat16 [768, 3072], replicated, may hold values from -0.21875 to 0.21875
- w_down: bfloat16 [3072, 768], replicated, may hold values from -0.109375 to 0.109375
- cotangent: bfloat16 [8, 512, 6, 768], P('dp', 'seq'), may hold values from -6 to 6
Outputs:
- layer_out: bfloat16 [8, 512, 6, 768], P('dp', 'seq')
- grad_tokens: bfloat16 [8, 512, 6, 768], P('dp', 'seq')
- grad_ln1: float32 [768], P('seq')
- grad_w_in: float32 [768, 2304], P('seq')
- grad_short_taps: float32 [3, 2304], P(None, 'seq')
- grad_cond_taps: float32 [3, 768], P(None, 'seq')
- grad_w_cond: float32 [768, 768], P('seq')
- grad_cond_bias: float32 [768], P('seq')
- grad_w_out: float32 [768, 768], P('seq')
- grad_ln2: float32 [768], P('seq')
- grad_gate: float32 [768, 3072], P('seq')
- grad_up: float32 [768, 3072], P('seq')
- grad_down: float32 [3072, 768], P('seq')
Inputs may be any that keep to these rules, and one draw needn't show every extreme that they name: Exactly 4 groups have kind 1.
All inputs are finite; a program needn't handle non-finite values.
Results may differ from a plain program's by a relative error of at most 0.017.
Values may be sent and summed in bfloat16 or wider, within the bound.
A program may use at most 256 MiB of HBM per device.

v0:
```python
import math
import jax
import jax.numpy as jnp
from jax import lax
from jax.sharding import PartitionSpec as P

highest = lax.Precision.HIGHEST
epsilon = 1e-05


def from_behind(value, axis, by):
    peers = lax.axis_size(axis)
    pairs = [(i, i + by) for i in range(peers) if 0 <= i + by < peers]
    return lax.ppermute(value, axis, pairs)


def norm_rows(values, scale_gain):
    row_mean = jnp.mean(values, axis=-1, keepdims=True)
    centered = values - row_mean
    scale_inv = lax.rsqrt(jnp.mean(centered * centered, axis=-1, keepdims=True) + epsilon)
    normed = centered * scale_inv
    return (normed * scale_gain, normed, scale_inv)


def norm_back(grad_out, normed, scale_inv, scale_gain):
    grad_gain = jnp.sum(grad_out * normed, axis=0)
    grad_normed = grad_out * scale_gain
    inner_mean = jnp.mean(grad_normed, axis=-1, keepdims=True)
    inner_cross = jnp.mean(grad_normed * normed, axis=-1, keepdims=True)
    return (scale_inv * (grad_normed - inner_mean - normed * inner_cross), grad_gain)


def wave_tables(freq_ids, time_ids, span_len):
    fold_freq = freq_ids[:, None] % span_len
    fold_time = time_ids[None, :] % span_len
    same_block = (freq_ids[:, None] // span_len == time_ids[None, :] // span_len).astype(
        jnp.float32
    )
    phase_index = fold_freq * fold_time % span_len
    phase_angle = phase_index.astype(jnp.float32) * (2.0 * math.pi) / span_len.astype(jnp.float32)
    return (jnp.cos(phase_angle) * same_block, jnp.sin(phase_angle) * same_block)


def conv_forward(extended, taps):
    return taps[0] * extended[2:] + taps[1] * extended[1:-1] + taps[2] * extended[:-2]


def conv_backward(grad_out, extended, taps, long_flag):
    count_rows = grad_out.shape[0]
    zero_pad = jnp.zeros((2,) + grad_out.shape[1:], jnp.float32)
    padded = jnp.concatenate([grad_out, zero_pad], axis=0)
    grad_local = (
        taps[0] * padded[:count_rows] + taps[1] * padded[1 : count_rows + 1] + taps[2] * padded[2:]
    )
    grad_rim = (
        jnp.stack([taps[2] * grad_out[0], taps[1] * grad_out[0] + taps[2] * grad_out[1]])
        * long_flag
    )
    grad_taps = jnp.stack(
        [
            jnp.sum(grad_out * extended[2:], axis=(0, 1)),
            jnp.sum(grad_out * extended[1:-1], axis=(0, 1)),
            jnp.sum(grad_out * extended[:-2], axis=(0, 1)),
        ]
    )
    return (grad_local, grad_rim, grad_taps)


def on_device(
    tokens,
    kind,
    ln1_gain,
    w_in,
    short_taps,
    cond_taps,
    w_cond,
    cond_bias,
    w_out,
    ln2_gain,
    w_gate,
    w_up,
    w_down,
    cotangent,
):
    piece_rows = tokens.shape[1]
    slot_count = tokens.shape[2]
    model_width = tokens.shape[3]
    flat_rows = piece_rows * slot_count
    seq_count = lax.axis_size("seq")
    seq_rank = lax.axis_index("seq")
    is_long = kind[0]
    long_flag = is_long.astype(jnp.float32)
    span_len = jnp.where(is_long == 1, piece_rows * seq_count, piece_rows).astype(jnp.int32)
    span_float = span_len.astype(jnp.float32)
    freq_ids = seq_rank * piece_rows + jnp.arange(piece_rows, dtype=jnp.int32)
    token_rows = tokens.reshape(flat_rows, model_width).astype(jnp.float32)
    normed_one, unit_one, inv_one = norm_rows(token_rows, ln1_gain)
    normed_one_low = normed_one.astype(jnp.bfloat16)
    projected = jnp.dot(normed_one_low, w_in, preferred_element_type=jnp.float32)
    proj_low = projected.astype(jnp.bfloat16).reshape(piece_rows, slot_count, 3 * model_width)
    proj_f = proj_low.astype(jnp.float32)
    rim_proj = from_behind(proj_low[piece_rows - 2 :], "seq", 1).astype(jnp.float32) * long_flag
    extended_proj = jnp.concatenate([rim_proj, proj_f], axis=0)
    conv_out = conv_forward(extended_proj, short_taps)
    query_conv = conv_out[:, :, :model_width]
    key_conv = conv_out[:, :, model_width : 2 * model_width]
    value_low = conv_out[:, :, 2 * model_width :].astype(jnp.bfloat16)
    value_f = value_low.astype(jnp.float32)
    rim_value = from_behind(value_low[piece_rows - 2 :], "seq", 1).astype(jnp.float32) * long_flag
    extended_value = jnp.concatenate([rim_value, value_f], axis=0)
    cond_low = conv_forward(extended_value, cond_taps).astype(jnp.bfloat16)
    signal_low = (key_conv * value_f).astype(jnp.bfloat16)
    sig_piece = lax.all_gather(signal_low, "seq", axis=0, tiled=True).astype(jnp.float32)
    cond_piece = lax.all_gather(cond_low, "seq", axis=0, tiled=True).astype(jnp.float32)
    time_ids = jnp.arange(sig_piece.shape[0], dtype=jnp.int32)
    cos_table, sin_table = wave_tables(freq_ids, time_ids, span_len)
    sig_cos = jnp.einsum("ft,tsd->fsd", cos_table, sig_piece, precision=highest)
    sig_sin = jnp.einsum("ft,tsd->fsd", sin_table, sig_piece, precision=highest)
    cond_cos = jnp.einsum("ft,tsd->fsd", cos_table, cond_piece, precision=highest)
    cond_sin = jnp.einsum("ft,tsd->fsd", sin_table, cond_piece, precision=highest)
    power_spec = (cond_cos * cond_cos + cond_sin * cond_sin) / span_float
    features_low = jnp.log1p(power_spec).astype(jnp.bfloat16).reshape(flat_rows, model_width)
    pre_tanh = jnp.dot(features_low, w_cond, preferred_element_type=jnp.float32) + cond_bias
    tanh_value = jnp.tanh(pre_tanh).reshape(piece_rows, slot_count, model_width)
    spectral_gain = 1.0 + tanh_value
    gained_cos = spectral_gain * sig_cos
    gained_sin = spectral_gain * sig_sin
    time_ids = jnp.arange(piece_rows * lax.axis_size("seq"), dtype=jnp.int32)
    cos_table, sin_table = wave_tables(freq_ids, time_ids, span_len)
    term = jnp.einsum("ft,fsd->tsd", cos_table, gained_cos, precision=highest) + jnp.einsum(
        "ft,fsd->tsd", sin_table, gained_sin, precision=highest
    )
    filtered = lax.psum_scatter(
        (term / span_float).astype(jnp.bfloat16), "seq", scatter_dimension=0, tiled=True
    ).astype(jnp.float32)
    mixed_low = (query_conv * filtered).astype(jnp.bfloat16).reshape(flat_rows, model_width)
    hidden_one = token_rows + jnp.dot(mixed_low, w_out, preferred_element_type=jnp.float32)
    normed_two, unit_two, inv_two = norm_rows(hidden_one, ln2_gain)
    normed_two_low = normed_two.astype(jnp.bfloat16)
    gate_pre = jnp.dot(normed_two_low, w_gate, preferred_element_type=jnp.float32)
    up_proj = jnp.dot(normed_two_low, w_up, preferred_element_type=jnp.float32)
    gate_sig = jax.nn.sigmoid(gate_pre)
    gate_act = gate_pre * gate_sig
    hidden_act = (gate_act * up_proj).astype(jnp.bfloat16)
    layer_rows = hidden_one + jnp.dot(hidden_act, w_down, preferred_element_type=jnp.float32)
    layer_out = layer_rows.astype(jnp.bfloat16).reshape(tokens.shape)
    cot_rows = cotangent.reshape(flat_rows, model_width)
    grad_down = jnp.einsum("nf,nd->fd", hidden_act, cot_rows, preferred_element_type=jnp.float32)
    grad_act = jnp.einsum("nd,fd->nf", cot_rows, w_down, preferred_element_type=jnp.float32)
    grad_gate_pre = (grad_act * up_proj * gate_sig * (1.0 + gate_pre * (1.0 - gate_sig))).astype(
        jnp.bfloat16
    )
    grad_up_proj = (grad_act * gate_act).astype(jnp.bfloat16)
    grad_gate = jnp.einsum(
        "nd,nf->df", normed_two_low, grad_gate_pre, preferred_element_type=jnp.float32
    )
    grad_up = jnp.einsum(
        "nd,nf->df", normed_two_low, grad_up_proj, preferred_element_type=jnp.float32
    )
    grad_normed_two = jnp.einsum(
        "nf,df->nd", grad_gate_pre, w_gate, preferred_element_type=jnp.float32
    ) + jnp.einsum("nf,df->nd", grad_up_proj, w_up, preferred_element_type=jnp.float32)
    grad_hidden_part, grad_ln2 = norm_back(grad_normed_two, unit_two, inv_two, ln2_gain)
    grad_hidden = cot_rows.astype(jnp.float32) + grad_hidden_part
    grad_mix_low = grad_hidden.astype(jnp.bfloat16)
    grad_w_out = jnp.einsum(
        "nd,ne->de", mixed_low, grad_mix_low, preferred_element_type=jnp.float32
    )
    grad_mixed = jnp.einsum(
        "ne,de->nd", grad_mix_low, w_out, preferred_element_type=jnp.float32
    ).reshape(piece_rows, slot_count, model_width)
    grad_query = grad_mixed * filtered
    grad_filtered_low = (grad_mixed * query_conv).astype(jnp.bfloat16)
    grad_piece = lax.all_gather(grad_filtered_low, "seq", axis=0, tiled=True).astype(jnp.float32)
    time_ids = jnp.arange(grad_piece.shape[0], dtype=jnp.int32)
    cos_table, sin_table = wave_tables(freq_ids, time_ids, span_len)
    back_cos = jnp.einsum("ft,tsd->fsd", cos_table, grad_piece, precision=highest)
    back_sin = jnp.einsum("ft,tsd->fsd", sin_table, grad_piece, precision=highest)
    back_cos = back_cos / span_float
    back_sin = back_sin / span_float
    grad_gain_spec = back_cos * sig_cos + back_sin * sig_sin
    grad_sig_cos = spectral_gain * back_cos
    grad_sig_sin = spectral_gain * back_sin
    grad_pre_low = (
        (grad_gain_spec * (1.0 - tanh_value * tanh_value))
        .astype(jnp.bfloat16)
        .reshape(flat_rows, model_width)
    )
    grad_w_cond = jnp.einsum(
        "nc,nd->cd", features_low, grad_pre_low, preferred_element_type=jnp.float32
    )
    grad_cond_bias = jnp.sum(grad_pre_low.astype(jnp.float32), axis=0)
    grad_features = jnp.einsum(
        "nd,cd->nc", grad_pre_low, w_cond, preferred_element_type=jnp.float32
    ).reshape(piece_rows, slot_count, model_width)
    grad_power = grad_features / (1.0 + power_spec)
    grad_cond_cos = 2.0 * cond_cos * grad_power / span_float
    grad_cond_sin = 2.0 * cond_sin * grad_power / span_float
    time_ids = jnp.arange(piece_rows * lax.axis_size("seq"), dtype=jnp.int32)
    cos_table, sin_table = wave_tables(freq_ids, time_ids, span_len)
    signal_term = jnp.einsum(
        "ft,fsd->tsd", cos_table, grad_sig_cos, precision=highest
    ) + jnp.einsum("ft,fsd->tsd", sin_table, grad_sig_sin, precision=highest)
    cond_term = jnp.einsum("ft,fsd->tsd", cos_table, grad_cond_cos, precision=highest) + jnp.einsum(
        "ft,fsd->tsd", sin_table, grad_cond_sin, precision=highest
    )
    source_grads = lax.psum_scatter(
        jnp.concatenate([signal_term, cond_term], axis=2).astype(jnp.bfloat16),
        "seq",
        scatter_dimension=0,
        tiled=True,
    ).astype(jnp.float32)
    grad_signal = source_grads[:, :, :model_width]
    grad_cond = source_grads[:, :, model_width:]
    grad_value_cond, grad_value_rim, grad_cond_taps = conv_backward(
        grad_cond, extended_value, cond_taps, long_flag
    )
    grad_value = grad_signal * key_conv + grad_value_cond
    grad_key = grad_signal * value_f
    value_back = from_behind(grad_value_rim.astype(jnp.bfloat16), "seq", -1).astype(
        grad_value_rim.dtype
    )
    grad_value = jnp.concatenate(
        [grad_value[: piece_rows - 2], grad_value[piece_rows - 2 :] + value_back], axis=0
    )
    grad_conv = jnp.concatenate([grad_query, grad_key, grad_value], axis=2)
    grad_proj_local, grad_proj_rim, grad_short_taps = conv_backward(
        grad_conv, extended_proj, short_taps, long_flag
    )
    proj_back = from_behind(grad_proj_rim.astype(jnp.bfloat16), "seq", -1).astype(
        grad_proj_rim.dtype
    )
    grad_proj = jnp.concatenate(
        [grad_proj_local[: piece_rows - 2], grad_proj_local[piece_rows - 2 :] + proj_back], axis=0
    )
    grad_proj_low = grad_proj.astype(jnp.bfloat16).reshape(flat_rows, 3 * model_width)
    grad_w_in = jnp.einsum(
        "nd,ne->de", normed_one_low, grad_proj_low, preferred_element_type=jnp.float32
    )
    grad_normed_one = jnp.einsum(
        "ne,de->nd", grad_proj_low, w_in, preferred_element_type=jnp.float32
    )
    grad_token_part, grad_ln1 = norm_back(grad_normed_one, unit_one, inv_one, ln1_gain)
    grad_tokens = (grad_hidden + grad_token_part).astype(jnp.bfloat16).reshape(tokens.shape)
    whole_sums = lax.psum(
        (
            grad_ln1,
            grad_w_in,
            grad_short_taps,
            grad_cond_taps,
            grad_w_cond,
            grad_cond_bias,
            grad_w_out,
            grad_ln2,
            grad_gate,
            grad_up,
            grad_down,
        ),
        ("dp", "seq"),
    )
    seq_dims = (0, 0, 1, 1, 0, 0, 0, 0, 0, 0, 0)
    summed = tuple(
        (
            lax.dynamic_slice_in_dim(
                whole_sum,
                seq_rank * (whole_sum.shape[axis_dim] // seq_count),
                whole_sum.shape[axis_dim] // seq_count,
                axis_dim,
            )
            for whole_sum, axis_dim in zip(whole_sums, seq_dims)
        )
    )
    return (
        layer_out,
        grad_tokens,
        summed[0],
        summed[1],
        summed[2],
        summed[3],
        summed[4],
        summed[5],
        summed[6],
        summed[7],
        summed[8],
        summed[9],
        summed[10],
    )


def solution(mesh):
    return jax.shard_map(
        on_device,
        mesh=mesh,
        in_specs=(
            P("dp", "seq", None, None),
            P("dp"),
            P(),
            P(),
            P(),
            P(),
            P(),
            P(),
            P(),
            P(),
            P(),
            P(),
            P(),
            P("dp", "seq", None, None),
        ),
        out_specs=(
            P("dp", "seq", None, None),
            P("dp", "seq", None, None),
            P("seq"),
            P("seq", None),
            P(None, "seq"),
            P(None, "seq"),
            P("seq", None),
            P("seq"),
            P("seq", None),
            P("seq"),
            P("seq", None),
            P("seq", None),
            P("seq", None),
        ),
        check_vma=False,
    )
```

profile of v0, /device:TPU:0, one launch (start us, length us, event | category | flops | bytes accessed | tf_op | source)
XLA Modules:
  0.0 1427.0 jit_solution(9233570854723160421)
XLA Ops:
  12.5 3.9 reshape.284
  19.1 5.5 convolution_convert_fusion
  30.1 5.5 collective-permute-start
  38.7 6.8 reshape.285
  45.5 6.0 copy.77
  63.7 89.3 %all-gather.4.cloned.1.call-done = bf16[512,6,768]{2,0,1:T(8,128)(2,1)} async-done(((bf16[128,6,768]{2,0,1:T(8,128)(2,1)}), bf16[512,6,768]{2,0,1:T(8,128)(2,1)}) %all-gather.4.cloned.1.call-update) | async-done | bytes 4718608 | tf_op jit(solution)/shard_map/all_gather | solution.py:114
  153.0 8.0 fusion.64
  161.0 8.2 log-plus-one_convert_fusion
  175.3 5.0 multiply_subtract_fusion
  183.9 59.2 %all-gather.6.cloned.1.call-done = bf16[512,6,768]{2,0,1:T(8,128)(2,1)} async-done(((bf16[128,6,768]{2,0,1:T(8,128)(2,1)}), bf16[512,6,768]{2,0,1:T(8,128)(2,1)}) %all-gather.6.cloned.1.call-update) | async-done | bytes 4718608 | tf_op jit(solution)/shard_map/all_gather | solution.py:113
  243.1 7.8 fusion.62
  251.0 11.7 fusion.26
  262.7 5.5 fusion.54
  269.6 14.8 %divide_convert_fusion = bf16[512,6,768]{2,0,1:T(8,128)(2,1)} fusion(f32[512,6,768]{2,0,1:T(8,128)S(1)} %fusion.26, f32[]{:T(128)S(6)} %convert_element_type.160, f32[128,6,768]{2,0,1:T(8,128)S(1)} %fusion.54, f32[128,6,768]{2,1,0:T(8,128)S(1)} %copy-done.2, s32[]{:T(128)S(6)} %select_n.103, s32[512]{0:T(512)S(1)} %get-tuple-element.107, ...), kind=kOutput, calls=%fused_computation.8 | convolution fusion | flops 3632332800 | bytes 18879496 | tf_op jit(solution)/shard_map/ft,fsd->tsd/dot_general | solution.py:130
  291.1 77.2 %reduce-scatter.3.cloned.1.call-done = bf16[128,6,768]{2,0,1:T(8,128)(2,1)} async-done(((bf16[512,6,768]{2,0,1:T(8,128)(2,1)}), bf16[128,6,768]{2,0,1:T(8,128)(2,1)}) %reduce-scatter.3.cloned.1.call-update) | async-done | bytes 1179664 | tf_op jit(solution)/shard_map/reduce_scatter | solution.py:133
  380.3 9.2 fusion.142
  389.5 6.2 fusion.143
  395.8 17.3 %multiply_convert_fusion = (bf16[768,3072]{1,0:T(8,128)(2,1)}, bf16[768,3072]{1,0:T(8,128)(2,1)}, bf16[768,3072]{1,0:T(8,128)(2,1)}) fusion(f32[768,3072]{1,0:T(8,128)} %fusion.142, f32[768,3072]{1,0:T(8,128)} %fusion.143, bf16[768,768]{1,0:T(8,128)(2,1)S(1)} %copy-done.31, bf16[3072,768]{1,0:T(8,128)(2,1)} %param.26), kind=kOutput, calls=%fused_computation.3 | convolution fusion | flops 3659268096 | bytes 38928384 | tf_op jit(solution)/shard_map/nd,fd->nf/dot_general | solution.py:149
  413.1 7.7 fusion.144
  420.9 7.3 multiply_reduce_fusion.2
  436.8 5.7 convert_multiply_fusion
  446.3 86.3 %all-gather.8.cloned.1.call-done = bf16[512,6,768]{2,0,1:T(8,128)(2,1)} async-done(((bf16[128,6,768]{2,0,1:T(8,128)(2,1)}), bf16[512,6,768]{2,0,1:T(8,128)(2,1)}) %all-gather.8.cloned.1.call-update) | async-done | bytes 4718608 | tf_op jit(solution)/shard_map/all_gather | solution.py:174
  532.6 7.9 convolution_divide_fusion.1
  540.6 11.6 fusion.23
  552.3 9.2 convert_reduce_fusion
  561.5 4.3 add_divide_fusion.1
  565.7 11.2 fusion.18
  577.0 15.4 %add_convert_fusion = bf16[512,6,768]{2,0,1:T(8,128)(2,1)} fusion(f32[512,6,768]{2,0,1:T(8,128)S(1)} %fusion.18, f32[128,6,768]{2,0,1:T(8,128)S(1)} %add_divide_fusion.1, f32[128,6,768]{2,0,1:T(8,128)} %get-tuple-element.101, f32[]{:T(128)S(6)} %convert_element_type.160, s32[]{:T(128)S(6)} %select_n.103, s32[512]{0:T(512)S(1)} %get-tuple-element.107, ...), kind=kOutput, calls=%fused_computation.1 | convolution fusion | flops 3631153152 | bytes 18879496 | tf_op jit(solution)/shard_map/ft,fsd->tsd/dot_general | solution.py:204
  592.3 15.3 %add_convert_fusion.1 = bf16[512,6,768]{2,0,1:T(8,128)(2,1)S(1)} fusion(f32[512,6,768]{2,0,1:T(8,128)S(1)} %fusion.23, f32[128,6,768]{2,0,1:T(8,128)} %get-tuple-element.105, f32[128,6,768]{2,1,0:T(8,128)S(1)} %copy-done.3, f32[]{:T(128)S(6)} %convert_element_type.160, s32[]{:T(128)S(6)} %select_n.103, s32[512]{0:T(512)S(1)} %get-tuple-element.107, ...), kind=kOutput, calls=%fused_computation.2 | convolution fusion | flops 3629973504 | bytes 18879496 | tf_op jit(solution)/shard_map/ft,fsd->tsd/dot_general | solution.py:203
  607.6 4.4 pad_maximum_fusion
  619.9 4.7 fusion.41
  624.6 8.8 fusion.146
  633.5 6.3 fusion.147
  639.8 6.3 fusion.148
  648.8 123.1 %reduce-scatter.5.cloned.1.call-done = bf16[128,6,1536]{2,0,1:T(8,128)(2,1)} async-done(((bf16[512,6,1536]{2,0,1:T(8,128)(2,1)}), bf16[128,6,1536]{2,0,1:T(8,128)(2,1)}) %reduce-scatter.5.cloned.1.call-update) | async-done | bytes 2359312 | tf_op jit(solution)/shard_map/reduce_scatter | solution.py:207
  776.2 4.2 multiply_reduce_fusion.4
  780.8 4.6 multiply_reduce_fusion.1
  792.7 4.1 copy.96
  796.8 6.6 convert_element_type.184
  803.4 8.2 fusion.145
  811.7 4.9 copy.98
  816.6 10.0 add_convert_fusion.3
  832.5 4.1 concatenate.42
  836.5 4.8 copy.99
  841.3 3.9 concatenate.43
  858.6 4.9 fusion.6
  876.4 44.4 %all-reduce.2 = (f32[768]{0:T(1024)}, f32[3,2304]{1,0:T(4,128)}, f32[3,768]{1,0:T(4,128)}, f32[768]{0:T(1024)}, f32[768]{0:T(1024)}) all-reduce(f32[768]{0:T(1024)} %get-tuple-element.58, f32[3,2304]{1,0:T(4,128)} %pad_maximum_fusion.4, f32[3,768]{1,0:T(4,128)S(1)} %copy-done.56, ...), channel_id=1, replica_groups=mesh['dp'=8,'seq'=4] {'dp','seq'}, use_global_device_ids=true, to_apply=%region_11.12 | all-reduce | flops 11520 | bytes 92160 | tf_op jit(solution)/shard_map/psum | solution.py:245
  927.5 476.0 %all-reduce.6.cloned.1.call-done = (f32[768,2304]{1,0:T(8,128)}, f32[768,768]{1,0:T(8,128)}, f32[768,768]{1,0:T(8,128)}, f32[768,3072]{1,0:T(8,128)}, f32[768,3072]{1,0:T(8,128)}, /*index=5*/f32[3072,768]{1,0:T(8,128)}) async-done(((f32[768,2304]{1,0:T(8,128)}, f32[768,768]{1,0:T(8,128)}, f32[768,768]{1,0:T(8,128)}, f32[768,3072]{1,0:T(8,128)}, f32[768,3072]{1,0:T(8,128)}, ...) | async-done | bytes 40108048 | tf_op jit(solution)/shard_map/psum | solution.py:245
  (277 shorter events, 147.6 us)
Async XLA Ops:
  7.2 11.9 copy-start
  7.2 145.8 %all-gather.4.cloned.1.call-start = ((), (), s32[]{:S(2)}) async-start(), calls=%async_computation.2 | async-start | bytes 5898240 | tf_op jit(solution)/shard_map/all_gather | solution.py:114
  12.5 6.6 copy-start.63
  16.4 8.2 copy-start.57
  18.1 6.5 copy-start.65
  30.1 22.0 %collective-permute-start = (bf16[2,6,2304]{2,0,1:T(2,128)(2,1)}, bf16[2,6,2304]{2,0,1:T(2,128)(2,1)}, u32[]{:S(2)}, u32[]{:S(2)}) collective-permute-start(bf16[2,6,2304]{2,0,1:T(2,128)(2,1)} %copy.78), channel_id=1, source_target_pairs={{0,1},{1,2},{2,3},{4,5},{5,6},{6,7},{8,9},{9,10},{10,11},{12,13},{... | collective-permute-start | bytes 165896 | tf_op jit(solution)/shard_map/ppermute | solution.py:14
  37.2 15.8 %copy-start.44 = (f32[2304]{0:T(1024)}, f32[2304]{0:T(1024)S(1)}, u32[]{:S(2)}) copy-start(f32[2304]{0:T(1024)S(1)} %get-tuple-element.64) | copy-start | bytes 27652
  38.7 21.7 %copy-start.52 = (f32[768]{0:T(1024)}, f32[768]{0:T(1024)S(1)}, u32[]{:S(2)}) copy-start(f32[768]{0:T(1024)S(1)} %get-tuple-element.67) | copy-start | bytes 9220
  45.5 7.6 copy-start.46
  45.5 7.6 copy-start.48
  55.8 6.7 copy-start.4
  55.9 4.5 collective-permute-start.1
  62.5 180.6 %all-gather.6.cloned.1.call-start = ((), (), s32[]{:S(2)}) async-start(), calls=%async_computation.3 | async-start | bytes 5898240 | tf_op jit(solution)/shard_map/all_gather | solution.py:113
  63.2 305.1 %reduce-scatter.3.cloned.1.call-start = ((), (), s32[]{:S(2)}) async-start(), calls=%async_computation.4 | async-start | bytes 5898240 | tf_op jit(solution)/shard_map/reduce_scatter | solution.py:133
  153.0 8.0 copy-start.33
  161.0 8.2 copy-start.27
  243.1 7.8 copy-start.2
  243.1 19.6 %slice-start.2 = ((s8[4718592]{0:T(1024)(128)(4,1)}), s8[4194304]{0:T(1024)(128)(4,1)S(1)}, s32[]{:S(2)}) async-start(s8[4718592]{0:T(1024)(128)(4,1)} %bitcast.76), calls=%async_computation.10 | async-start | bytes 8388608
  251.0 11.7 copy-start.7
  251.0 11.7 slice-start.3
  284.5 248.1 %all-gather.8.cloned.1.call-start = ((), (), s32[]{:S(2)}) async-start(), calls=%async_computation.5 | async-start | bytes 5898240 | tf_op jit(solution)/shard_map/all_gather | solution.py:174
  379.2 49.0 %copy-start.5 = (f32[768,768]{1,0:T(8,128)}, f32[768,768]{1,0:T(8,128)S(1)}, u32[]{:S(2)}) copy-start(f32[768,768]{1,0:T(8,128)S(1)} %get-tuple-element.103) | copy-start | bytes 7077892
  379.9 9.6 slice-start.8
  380.2 9.3 copy-start.22
  380.3 9.3 slice-start.9
  389.5 6.3 copy-start.31
  413.1 7.8 copy-start.34
  442.5 329.4 %reduce-scatter.5.cloned.1.call-start = ((), (), s32[]{:S(2)}) async-start(), calls=%async_computation.6 | async-start | bytes 11796480 | tf_op jit(solution)/shard_map/reduce_scatter | solution.py:207
  532.6 8.0 copy-start.3
  532.6 19.6 %slice-start.4 = ((s8[4718592]{0:T(1024)(128)(4,1)}), s8[4194304]{0:T(1024)(128)(4,1)S(1)}, s32[]{:S(2)}) async-start(s8[4718592]{0:T(1024)(128)(4,1)} %bitcast.78), calls=%async_computation.12 | async-start | bytes 8388608
  540.5 11.7 copy-start.8
  540.6 11.7 copy-start.24
  540.6 11.7 copy-start.26
  540.6 11.7 slice-start.5
  552.3 9.2 copy-start.28
  592.3 15.3 %copy-start.18 = (bf16[512,6,768]{2,0,1:T(8,128)(2,1)S(1)}, bf16[512,6,768]{2,0,1:T(8,128)(2,1)}, u32[]{:S(2)}) copy-start(bf16[512,6,768]{2,0,1:T(8,128)(2,1)} %add_convert_fusion) | copy-start | bytes 14155780
  612.0 791.5 %all-reduce.6.cloned.1.call-start = ((), (), s32[]{:S(2)}) async-start(), calls=%async_computation.7 | async-start | bytes 80216064 | tf_op jit(solution)/shard_map/psum | solution.py:245
  619.9 13.5 slice-start.6
  624.6 8.8 slice-start.7
  624.6 15.2 %slice-start.10 = ((s8[4718592]{0:T(1024)(128)(4,1)}), s8[4194304]{0:T(1024)(128)(4,1)S(1)}, s32[]{:S(2)}) async-start(s8[4718592]{0:T(1024)(128)(4,1)} %bitcast.84), calls=%async_computation.18 | async-start | bytes 8388608
  633.5 6.3 copy-start.32
  633.5 6.3 slice-start.11
  639.8 6.4 copy-start.36
  639.8 6.4 copy-start.38
  648.8 125.6 %copy-start.53 = (f32[768]{0:T(1024)S(1)}, f32[768]{0:T(1024)}, u32[]{:S(2)}) copy-start(f32[768]{0:T(1024)} %copy-done.52) | copy-start | bytes 9220
  648.8 125.6 %copy-start.55 = (f32[768]{0:T(1024)S(1)}, f32[768]{0:T(1024)}, u32[]{:S(2)}) copy-start(f32[768]{0:T(1024)} %get-tuple-element.68) | copy-start | bytes 9220
  774.5 5.9 collective-permute-start.2
  785.6 6.8 collective-permute-start.3
  (45 other events, 172.8 us)
Sparse Core Ops, SparseCore 0:
  62.6 90.3 all-gather.3
  155.2 87.9 all-gather.5
  284.6 83.6 reduce-scatter.2
  442.6 89.9 all-gather.7
  612.1 159.7 reduce-scatter.4
  811.8 591.6 all-reduce.5
where the time goes:
time: 1440 us; the launch traced here: 1430 us
  waiting for transfers between devices  916 us (64%)
  matrix products  246 us (17%)
  local copies, waits for them, and re-layouts  146 us (10%)
  other arithmetic  46.6 us (3%)
  blocking collectives  44.4 us (3%)
  between operations  16.2 us (1%)
    psum x1, waiting for transfers between devices, on_device(): lax.psum((grad_ln1, grad_w_in, grad_short_taps, grad_cond_taps, grad_w_co...  476 us
    reduce_scatter x1, waiting for transfers between devices, on_device(): lax.psum_scatter(jnp.concatenate([signal_term, cond_term], axis=2).astype...  123 us
    all_gather x1, waiting for transfers between devices, on_device(): lax.all_gather(cond_low, 'seq', axis=0, tiled=True).astype(jnp.float32)  89.3 us
    all_gather x1, waiting for transfers between devices, on_device(): lax.all_gather(grad_filtered_low, 'seq', axis=0, tiled=True)  86.3 us
    reduce_scatter x1, waiting for transfers between devices, on_device(): lax.psum_scatter((term / span_float).astype(jnp.bfloat16), 'seq', scatter...  77.2 us
    all_gather x1, waiting for transfers between devices, on_device(): lax.all_gather(signal_low, 'seq', axis=0, tiled=True).astype(jnp.float32)  59.2 us
    psum x1, blocking collectives, on_device(): lax.psum((grad_ln1, grad_w_in, grad_short_taps, grad_cond_taps, grad_w_co...  44.4 us
  transfers between devices with their start and end apart: 10, of which 8 were waited for; matrix products, arithmetic and copies ran while one was open for 12% of the time, Pallas kernels for 0%

commit v1 on v0

--- a/solution.py
+++ b/solution.py
@@ -6,6 +6,18 @@
 
 highest = lax.Precision.HIGHEST
 epsilon = 1e-05
+
+
+def gather_by_bits(x, axis, dim):
+    ways, here = (lax.axis_size(axis), lax.axis_index(axis))
+    grown, reach = (x, 1)
+    while reach < ways:
+        theirs = lax.ppermute(grown, axis, [(d, d ^ reach) for d in range(ways)])
+        mine_first = jnp.concatenate([grown, theirs], axis=dim)
+        theirs_first = jnp.concatenate([theirs, grown], axis=dim)
+        grown = jnp.where(here & reach == 0, mine_first, theirs_first)
+        reach = 2 * reach
+    return grown
 
 
 def from_behind(value, axis, by):
@@ -111,7 +123,7 @@
     cond_low = conv_forward(extended_value, cond_taps).astype(jnp.bfloat16)
     signal_low = (key_conv * value_f).astype(jnp.bfloat16)
     sig_piece = lax.all_gather(signal_low, "seq", axis=0, tiled=True).astype(jnp.float32)
-    cond_piece = lax.all_gather(cond_low, "seq", axis=0, tiled=True).astype(jnp.float32)
+    cond_piece = gather_by_bits(cond_low, "seq", 0).astype(jnp.float32)
     time_ids = jnp.arange(sig_piece.shape[0], dtype=jnp.int32)
     cos_table, sin_table = wave_tables(freq_ids, time_ids, span_len)
     sig_cos = jnp.einsum("ft,tsd->fsd", cos_table, sig_piece, precision=highest)

time: 1440 us -> 1490 us (1.035)
  waiting for transfers between devices: 916 us -> 957 us
    ppermute x0 -> x2, waiting for transfers between devices: none -> 189 us  [gather_by_bits(): theirs = lax.ppermute(grown, axis, [(d, d ^ reach) for d in range(ways)])]
    all_gather x1 -> x0, waiting for transfers between devices: 89.3 us -> none  [on_device(): lax.all_gather(cond_low, 'seq', axis=0, tiled=True).astype(jnp.float32)]
    all_gather x1, waiting for transfers between devices: 59.2 us -> 0.01 us  [on_device(): lax.all_gather(signal_low, 'seq', axis=0, tiled=True).astype(jnp.float32)]
  transfers between devices with their start and end apart: 10 -> 11, of which waited for: 8 -> 8; matrix products, arithmetic and copies ran while one was open for 12% -> 12% of each run, Pallas kernels for 0% -> 0%
where the time goes in v1:
time: 1490 us; the launch traced here: 1480 us
  waiting for transfers between devices  957 us (64%)
  matrix products  254 us (17%)
  local copies, waits for them, and re-layouts  146 us (10%)
  other arithmetic  50.8 us (3%)
  blocking collectives  44.4 us (3%)
  between operations  15.8 us (1%)
    psum x1, waiting for transfers between devices, on_device(): lax.psum((grad_ln1, grad_w_in, grad_short_taps, grad_cond_taps, grad_w_co...  476 us
    ppermute x2, waiting for transfers between devices, gather_by_bits(): theirs = lax.ppermute(grown, axis, [(d, d ^ reach) for d in range(ways)])  189 us
    reduce_scatter x1, waiting for transfers between devices, on_device(): lax.psum_scatter(jnp.concatenate([signal_term, cond_term], axis=2).astype...  123 us
    all_gather x1, waiting for transfers between devices, on_device(): lax.all_gather(grad_filtered_low, 'seq', axis=0, tiled=True)  86.3 us
    reduce_scatter x1, waiting for transfers between devices, on_device(): lax.psum_scatter((term / span_float).astype(jnp.bfloat16), 'seq', scatter...  77.7 us
    psum x1, blocking collectives, on_device(): lax.psum((grad_ln1, grad_w_in, grad_short_taps, grad_cond_taps, grad_w_co...  44.4 us
  transfers between devices with their start and end apart: 11, of which 8 were waited for; matrix products, arithmetic and copies ran while one was open for 12% of the time, Pallas kernels for 0%

profile of v1, /device:TPU:0, one launch (start us, length us, event | category | flops | bytes accessed | tf_op | source)
XLA Modules:
  0.0 1482.0 jit_solution(1089705478494966883)
XLA Ops:
  19.1 5.5 convolution_convert_fusion
  30.1 5.5 collective-permute-start
  38.7 6.8 reshape.285
  45.5 6.0 copy.77
  64.9 73.6 %collective-permute-done.2 = bf16[128,6,768]{2,0,1:T(8,128)(2,1)} collective-permute-done((bf16[128,6,768]{2,0,1:T(8,128)(2,1)}, bf16[128,6,768]{2,0,1:T(8,128)(2,1)}, u32[]{:S(2)}, u32[]{:S(2)}) %collective-permute-start.2) | collective-permute-done | bytes 1179680 | tf_op jit(solution)/shard_map/ppermute | solution.py:15
  138.5 4.2 maximum_select_fusion.1
  143.7 115.9 %collective-permute-done.3 = bf16[256,6,768]{2,0,1:T(8,128)(2,1)} collective-permute-done((bf16[256,6,768]{2,0,1:T(8,128)(2,1)}, bf16[256,6,768]{2,0,1:T(8,128)(2,1)}, u32[]{:S(2)}, u32[]{:S(2)}) %collective-permute-start.3) | collective-permute-done | bytes 2359328 | tf_op jit(solution)/shard_map/ppermute | solution.py:15
  259.6 10.0 fusion.38
  269.7 13.6 log-plus-one_convert_fusion
  289.3 5.0 multiply_subtract_fusion
  297.8 7.8 fusion.63
  305.7 11.7 fusion.26
  317.4 5.5 fusion.56
  324.3 14.8 divide_convert_fusion
  345.8 77.7 %reduce-scatter.3.cloned.1.call-done = bf16[128,6,768]{2,0,1:T(8,128)(2,1)} async-done(((bf16[512,6,768]{2,0,1:T(8,128)(2,1)}), bf16[128,6,768]{2,0,1:T(8,128)(2,1)}) %reduce-scatter.3.cloned.1.call-update) | async-done | bytes 1179664 | tf_op jit(solution)/shard_map/reduce_scatter | solution.py:145
  435.5 9.2 fusion.144
  444.8 6.3 fusion.145
  451.1 17.3 %multiply_convert_fusion = (bf16[768,3072]{1,0:T(8,128)(2,1)}, bf16[768,3072]{1,0:T(8,128)(2,1)}, bf16[768,3072]{1,0:T(8,128)(2,1)}) fusion(f32[768,3072]{1,0:T(8,128)} %fusion.144, f32[768,3072]{1,0:T(8,128)} %fusion.145, bf16[768,768]{1,0:T(8,128)(2,1)S(1)} %copy-done.28, bf16[3072,768]{1,0:T(8,128)(2,1)} %param.26), kind=kOutput, calls=%fused_computation.3 | convolution fusion | flops 3659268096 | bytes 38928384 | tf_op jit(solution)/shard_map/nd,fd->nf/dot_general | solution.py:161
  468.5 7.7 fusion.146
  476.2 7.3 multiply_reduce_fusion.2
  492.2 5.7 convert_multiply_fusion
  501.7 86.3 %all-gather.5.cloned.1.call-done = bf16[512,6,768]{2,0,1:T(8,128)(2,1)} async-done(((bf16[128,6,768]{2,0,1:T(8,128)(2,1)}), bf16[512,6,768]{2,0,1:T(8,128)(2,1)}) %all-gather.5.cloned.1.call-update) | async-done | bytes 4718608 | tf_op jit(solution)/shard_map/all_gather | solution.py:186
  588.0 7.9 convolution_divide_fusion.1
  596.0 11.6 fusion.23
  607.7 9.2 convert_reduce_fusion
  616.8 4.2 add_divide_fusion.1
  621.1 11.2 fusion.18
  632.3 15.3 %add_convert_fusion = bf16[512,6,768]{2,0,1:T(8,128)(2,1)} fusion(f32[512,6,768]{2,0,1:T(8,128)S(1)} %fusion.18, f32[128,6,768]{2,0,1:T(8,128)S(1)} %add_divide_fusion.1, f32[128,6,768]{2,0,1:T(8,128)} %get-tuple-element.101, f32[]{:T(128)S(6)} %convert_element_type.160, s32[]{:T(128)S(6)} %select_n.119, s32[512]{0:T(512)S(1)} %get-tuple-element.107, ...), kind=kOutput, calls=%fused_computation.1 | convolution fusion | flops 3631153152 | bytes 18879496 | tf_op jit(solution)/shard_map/ft,fsd->tsd/dot_general | solution.py:216
  647.7 15.3 %add_convert_fusion.1 = bf16[512,6,768]{2,0,1:T(8,128)(2,1)S(1)} fusion(f32[512,6,768]{2,0,1:T(8,128)S(1)} %fusion.23, f32[128,6,768]{2,0,1:T(8,128)} %get-tuple-element.105, f32[128,6,768]{2,1,0:T(8,128)S(1)} %copy-done.3, f32[]{:T(128)S(6)} %convert_element_type.160, s32[]{:T(128)S(6)} %select_n.119, s32[512]{0:T(512)S(1)} %get-tuple-element.107, ...), kind=kOutput, calls=%fused_computation.2 | convolution fusion | flops 3629973504 | bytes 18879496 | tf_op jit(solution)/shard_map/ft,fsd->tsd/dot_general | solution.py:215
  662.9 4.4 pad_maximum_fusion
  675.3 4.7 fusion.43
  679.9 8.8 fusion.148
  688.8 6.4 fusion.149
  695.3 6.4 fusion.150
  704.3 123.0 %reduce-scatter.5.cloned.1.call-done = bf16[128,6,1536]{2,0,1:T(8,128)(2,1)} async-done(((bf16[512,6,1536]{2,0,1:T(8,128)(2,1)}), bf16[128,6,1536]{2,0,1:T(8,128)(2,1)}) %reduce-scatter.5.cloned.1.call-update) | async-done | bytes 2359312 | tf_op jit(solution)/shard_map/reduce_scatter | solution.py:219
  831.5 4.2 multiply_reduce_fusion.4
  836.1 4.6 multiply_reduce_fusion.1
  848.0 4.1 copy.96
  852.1 6.6 convert_element_type.184
  858.7 8.3 fusion.147
  867.0 4.9 copy.98
  871.9 10.0 add_convert_fusion.3
  887.8 4.1 concatenate.58
  891.9 4.8 copy.99
  896.7 3.9 concatenate.59
  914.0 4.9 fusion.6
  931.8 44.4 %all-reduce.2 = (f32[768]{0:T(1024)}, f32[3,2304]{1,0:T(4,128)}, f32[3,768]{1,0:T(4,128)}, f32[768]{0:T(1024)}, f32[768]{0:T(1024)}) all-reduce(f32[768]{0:T(1024)} %get-tuple-element.58, f32[3,2304]{1,0:T(4,128)} %pad_maximum_fusion.4, f32[3,768]{1,0:T(4,128)S(1)} %copy-done.55, ...), channel_id=1, replica_groups=mesh['dp'=8,'seq'=4] {'dp','seq'}, use_global_device_ids=true, to_apply=%region_11.12 | all-reduce | flops 11520 | bytes 92160 | tf_op jit(solution)/shard_map/psum | solution.py:257
  982.8 476.0 %all-reduce.6.cloned.1.call-done = (f32[768,2304]{1,0:T(8,128)}, f32[768,768]{1,0:T(8,128)}, f32[768,768]{1,0:T(8,128)}, f32[768,3072]{1,0:T(8,128)}, f32[768,3072]{1,0:T(8,128)}, /*index=5*/f32[3072,768]{1,0:T(8,128)}) async-done(((f32[768,2304]{1,0:T(8,128)}, f32[768,768]{1,0:T(8,128)}, f32[768,768]{1,0:T(8,128)}, f32[768,3072]{1,0:T(8,128)}, f32[768,3072]{1,0:T(8,128)}, ...) | async-done | bytes 40108048 | tf_op jit(solution)/shard_map/psum | solution.py:257
  (277 shorter events, 153.6 us)
Async XLA Ops:
  7.2 11.9 copy-start
  7.2 290.6 %all-gather.3.cloned.1.call-start = ((), (), s32[]{:S(2)}) async-start(), calls=%async_computation.2 | async-start | bytes 5898240 | tf_op jit(solution)/shard_map/all_gather | solution.py:125
  12.5 6.6 copy-start.62
  16.4 8.2 copy-start.56
  18.1 6.5 copy-start.64
  30.1 22.0 %collective-permute-start = (bf16[2,6,2304]{2,0,1:T(2,128)(2,1)}, bf16[2,6,2304]{2,0,1:T(2,128)(2,1)}, u32[]{:S(2)}, u32[]{:S(2)}) collective-permute-start(bf16[2,6,2304]{2,0,1:T(2,128)(2,1)} %copy.78), channel_id=1, source_target_pairs={{0,1},{1,2},{2,3},{4,5},{5,6},{6,7},{8,9},{9,10},{10,11},{12,13},{... | collective-permute-start | bytes 165896 | tf_op jit(solution)/shard_map/ppermute | solution.py:26
  37.2 15.8 %copy-start.43 = (f32[2304]{0:T(1024)}, f32[2304]{0:T(1024)S(1)}, u32[]{:S(2)}) copy-start(f32[2304]{0:T(1024)S(1)} %get-tuple-element.64) | copy-start | bytes 27652
  38.7 21.7 %copy-start.51 = (f32[768]{0:T(1024)}, f32[768]{0:T(1024)S(1)}, u32[]{:S(2)}) copy-start(f32[768]{0:T(1024)S(1)} %get-tuple-element.67) | copy-start | bytes 9220
  45.5 7.6 copy-start.45
  45.5 7.6 copy-start.47
  55.8 6.7 copy-start.4
  55.9 4.5 collective-permute-start.1
  62.5 361.0 %reduce-scatter.3.cloned.1.call-start = ((), (), s32[]{:S(2)}) async-start(), calls=%async_computation.3 | async-start | bytes 5898240 | tf_op jit(solution)/shard_map/reduce_scatter | solution.py:145
  62.5 75.9 %collective-permute-start.2 = (bf16[128,6,768]{2,0,1:T(8,128)(2,1)}, bf16[128,6,768]{2,0,1:T(8,128)(2,1)}, u32[]{:S(2)}, u32[]{:S(2)}) collective-permute-start(bf16[128,6,768]{2,0,1:T(8,128)(2,1)} %get-tuple-element.94), channel_id=1, source_target_pairs={{0,1},{1,0},{2,3},{3,2},{4,5},{5,4},{6,7},{7,6},{8,9},{9,8},{10,11... | collective-permute-start | bytes 3538952 | tf_op jit(solution)/shard_map/ppermute | solution.py:15
  142.7 116.9 %collective-permute-start.3 = (bf16[256,6,768]{2,0,1:T(8,128)(2,1)}, bf16[256,6,768]{2,0,1:T(8,128)(2,1)}, u32[]{:S(2)}, u32[]{:S(2)}) collective-permute-start(bf16[256,6,768]{2,0,1:T(8,128)(2,1)} %maximum_select_fusion.1), channel_id=1, source_target_pairs={{0,2},{1,3},{2,0},{3,1},{4,6},{5,7},{6,4},{7,5},{8,10},{9,11},{10,... | collective-permute-start | bytes 7077896 | tf_op jit(solution)/shard_map/ppermute | solution.py:15
  269.6 13.6 copy-start.33
  297.8 7.9 copy-start.2
  297.8 19.6 %slice-start.2 = ((s8[4718592]{0:T(1024)(128)(4,1)}), s8[4194304]{0:T(1024)(128)(4,1)S(1)}, s32[]{:S(2)}) async-start(s8[4718592]{0:T(1024)(128)(4,1)} %bitcast.74), calls=%async_computation.9 | async-start | bytes 8388608
  305.7 11.7 copy-start.7
  305.7 11.7 slice-start.3
  339.2 248.8 %all-gather.5.cloned.1.call-start = ((), (), s32[]{:S(2)}) async-start(), calls=%async_computation.4 | async-start | bytes 5898240 | tf_op jit(solution)/shard_map/all_gather | solution.py:186
  434.4 49.1 %copy-start.5 = (f32[768,768]{1,0:T(8,128)}, f32[768,768]{1,0:T(8,128)S(1)}, u32[]{:S(2)}) copy-start(f32[768,768]{1,0:T(8,128)S(1)} %get-tuple-element.103) | copy-start | bytes 7077892
  435.1 9.6 slice-start.8
  435.5 9.3 copy-start.22
  435.5 9.3 slice-start.9
  444.8 6.3 copy-start.28
  468.5 7.8 copy-start.30
  497.9 329.3 %reduce-scatter.5.cloned.1.call-start = ((), (), s32[]{:S(2)}) async-start(), calls=%async_computation.5 | async-start | bytes 11796480 | tf_op jit(solution)/shard_map/reduce_scatter | solution.py:219
  588.0 8.0 copy-start.3
  588.0 19.6 %slice-start.4 = ((s8[4718592]{0:T(1024)(128)(4,1)}), s8[4194304]{0:T(1024)(128)(4,1)S(1)}, s32[]{:S(2)}) async-start(s8[4718592]{0:T(1024)(128)(4,1)} %bitcast.76), calls=%async_computation.11 | async-start | bytes 8388608
  595.9 11.7 copy-start.8
  595.9 11.7 copy-start.24
  595.9 11.7 copy-start.26
  595.9 11.7 slice-start.5
  607.7 9.2 copy-start.32
  647.7 15.3 %copy-start.18 = (bf16[512,6,768]{2,0,1:T(8,128)(2,1)S(1)}, bf16[512,6,768]{2,0,1:T(8,128)(2,1)}, u32[]{:S(2)}) copy-start(bf16[512,6,768]{2,0,1:T(8,128)(2,1)} %add_convert_fusion) | copy-start | bytes 14155780
  667.3 791.5 %all-reduce.6.cloned.1.call-start = ((), (), s32[]{:S(2)}) async-start(), calls=%async_computation.6 | async-start | bytes 80216064 | tf_op jit(solution)/shard_map/psum | solution.py:257
  675.2 13.5 slice-start.6
  679.9 8.9 slice-start.7
  679.9 15.3 %slice-start.10 = ((s8[4718592]{0:T(1024)(128)(4,1)}), s8[4194304]{0:T(1024)(128)(4,1)S(1)}, s32[]{:S(2)}) async-start(s8[4718592]{0:T(1024)(128)(4,1)} %bitcast.82), calls=%async_computation.17 | async-start | bytes 8388608
  688.8 6.4 copy-start.29
  688.8 6.4 slice-start.11
  695.2 6.4 copy-start.35
  695.3 6.4 copy-start.37
  704.2 125.4 %copy-start.52 = (f32[768]{0:T(1024)S(1)}, f32[768]{0:T(1024)}, u32[]{:S(2)}) copy-start(f32[768]{0:T(1024)} %copy-done.51) | copy-start | bytes 9220
  704.2 125.4 %copy-start.54 = (f32[768]{0:T(1024)S(1)}, f32[768]{0:T(1024)}, u32[]{:S(2)}) copy-start(f32[768]{0:T(1024)} %get-tuple-element.68) | copy-start | bytes 9220
  829.8 5.9 collective-permute-start.4
  840.9 6.8 collective-permute-start.5
  (45 other events, 172.8 us)
Sparse Core Ops, SparseCore 0:
  62.6 132.2 all-gather.2
  339.3 84.1 reduce-scatter.2
  498.0 89.9 all-gather.4
  667.4 159.7 reduce-scatter.4
  867.1 591.6 all-reduce.5
